TPU v7x, 256 devices: a whole 4x4x8 slice. The times are simulated.
256 devices in a mesh: seq: 8 (over y, core), fsdp: 16 (over z_hi, x), tp: 2 (over z_lo).
Axes of the slice: x: 4, y: 4, z: 8 (z_hi: 4, z_lo: 2; z = z_hi * 2 + z_lo), core: 2. Of those that a mesh axis runs over, the one named last changes fastest.
Arguments:
- hidden: bfloat16 [16, 1024, 8192], P('fsdp', 'seq'), may hold values from -6 to 6
- queries: bfloat16 [16, 1024, 8192], P('fsdp', 'seq', 'tp'), may hold values from -600 to 600
- w_kv: bfloat16 [2, 8192, 1024], P(None, 'fsdp', 'tp'), may hold values from -0.0625 to 0.0625
- b_kv: bfloat16 [2, 1024], P(None, 'tp'), may hold values from -3 to 3
- doc_starts: int32 [16, 2], P('fsdp'), may hold values from 0 to 896, as said below
- block_docs: int32 [16, 8], P('fsdp'), may hold values from 0 to 1, as said below
Outputs:
- attended: bfloat16 [16, 1024, 8192], P('fsdp', 'seq', 'tp')
Inputs may be any that keep to these rules, and one draw needn't show every extreme that they name: `doc_starts`: each row holds exactly 2 documents of whole blocks of 128 tokens, starts rising from 0; one document of each row has exactly 6 blocks. `block_docs`: the document of each block, matching doc_starts.
All inputs are finite; a program needn't handle non-finite values.
Results may differ from a plain program's by a relative error of at most 0.015.
Values may be sent and summed in bfloat16 or wider, within the bound.
A program may use at most 128 MiB of HBM per device.

v0:
```python
import jax
import jax.numpy as jnp
from jax import lax
from jax.sharding import Mesh
from jax.sharding import PartitionSpec as P

HD = 128
BLK = 128
SEQ = ("sy", "sc")
FSDP = ("fz", "fx")


def rotate_keys(key_heads, positions):
    half = key_heads.shape[-1] // 2
    freqs = jnp.exp(
        -jnp.arange(half, dtype=jnp.float32)
        * (2.0 / key_heads.shape[-1])
        * jnp.log(jnp.float32(1000000.0))
    )
    angle = positions.astype(jnp.float32)[:, None] * freqs[None, :]
    cosine = jnp.cos(angle)[:, None, :]
    sine = jnp.sin(angle)[:, None, :]
    first = key_heads[..., :half]
    second = key_heads[..., half:]
    return jnp.concatenate(
        [first * cosine - second * sine, second * cosine + first * sine], axis=-1
    )


def lookup_docs(token_index, block_table):
    block_index = token_index // BLK
    matches = block_index[:, None] == jnp.arange(block_table.shape[0], dtype=jnp.int32)[None, :]
    return jnp.sum(jnp.where(matches, block_table[None, :], 0), axis=1)


def doc_positions(token_index, doc_starts, block_docs):
    docs = lookup_docs(token_index, block_docs[0])
    doc_match = docs[:, None] == jnp.arange(doc_starts.shape[1], dtype=jnp.int32)[None, :]
    doc_first = jnp.sum(jnp.where(doc_match, doc_starts[0][None, :], 0), axis=1)
    return (docs, token_index - doc_first)


def make_per_device(cores):

    def per_device(hidden, queries, w_kv, b_kv, doc_starts, block_docs):
        tok_count = hidden.shape[1]
        core = lax.axis_index("sc")
        chip = lax.axis_index("sy")
        cols = w_kv.shape[2] // cores
        w_part = lax.dynamic_slice_in_dim(w_kv, core * cols, cols, axis=2)
        b_part = lax.dynamic_slice_in_dim(b_kv, core * cols, cols, axis=1)
        chip_rows = lax.all_gather(hidden[0], "sc", axis=0, tiled=True)
        chip_tokens = chip_rows.shape[0]
        key_value = jnp.einsum(
            "td,cde->cte",
            chip_rows,
            lax.all_gather(w_part, FSDP, axis=1, tiled=True),
            preferred_element_type=jnp.float32,
        )
        key_value = key_value + b_part.astype(jnp.float32)[:, None, :]
        chip_pos = chip * chip_tokens + jnp.arange(chip_tokens, dtype=jnp.int32)
        _, positions = doc_positions(chip_pos, doc_starts, block_docs)
        part_heads = cols // HD
        rotated = rotate_keys(key_value[0].reshape(chip_tokens, part_heads, HD), positions)
        keys = rotated.astype(jnp.bfloat16).reshape(chip_tokens, cols)
        values = key_value[1].astype(jnp.bfloat16)
        stacked = jnp.stack([keys, values])
        gathered = lax.all_gather(stacked, SEQ, axis=0, tiled=False)
        chips = gathered.shape[0] // cores
        gathered = gathered.reshape(chips, cores, 2, chip_tokens, cols)
        piece = jnp.transpose(gathered, (2, 0, 3, 1, 4)).reshape(
            2, chips * chip_tokens, cores * cols
        )
        seq_pos = (chip * cores + core) * tok_count + jnp.arange(tok_count, dtype=jnp.int32)
        query_docs = lookup_docs(seq_pos, block_docs[0])
        key_heads = piece.shape[2] // HD
        group = queries.shape[2] // HD // key_heads
        query_heads = queries[0].reshape(tok_count, key_heads, group, HD)
        inv_root = 1.0 / jnp.sqrt(jnp.float32(HD))
        width = piece.shape[1]
        key_docs = lookup_docs(jnp.arange(width, dtype=jnp.int32), block_docs[0])
        same_doc = query_docs[:, None] == key_docs[None, :]
        run_max = jnp.full((key_heads, group, tok_count), -1e30, jnp.float32)
        key_part = piece[0].reshape(width, key_heads, HD)
        value_part = piece[1].reshape(width, key_heads, HD)
        scores = (
            jnp.einsum("tgjd,sgd->gjts", query_heads, key_part, preferred_element_type=jnp.float32)
            * inv_root
        )
        scores = jnp.where(same_doc[None, None], scores, jnp.float32(-1e30))
        new_max = jnp.maximum(run_max, jnp.max(scores, axis=-1))
        weight = jnp.where(
            same_doc[None, None], jnp.exp(scores - new_max[..., None]), jnp.float32(0.0)
        )
        new_sum = jnp.sum(weight, axis=-1)
        update = jnp.einsum(
            "gjts,sgd->gjtd",
            weight.astype(jnp.bfloat16),
            value_part,
            preferred_element_type=jnp.float32,
        )
        result = update / new_sum[..., None]
        result = jnp.transpose(result, (2, 0, 1, 3)).reshape(tok_count, key_heads * group * HD)
        return result.astype(jnp.bfloat16)[None]

    return per_device


def solution(mesh):
    seq, fsdp, tp = (mesh.shape[name] for name in ("seq", "fsdp", "tp"))
    cores = 2
    x_size = 4
    fine = Mesh(
        mesh.devices.reshape(seq // cores, cores, fsdp // x_size, x_size, tp),
        ("sy", "sc", "fz", "fx", "tp"),
    )
    in_specs = (
        P(FSDP, SEQ, None),
        P(FSDP, SEQ, "tp"),
        P(None, FSDP, "tp"),
        P(None, "tp"),
        P(FSDP, None),
        P(FSDP, None),
    )
    out_specs = P(FSDP, SEQ, "tp")
    return jax.shard_map(
        make_per_device(cores), mesh=fine, in_specs=in_specs, out_specs=out_specs, check_vma=False
    )
```

profile of v0, /device:TPU:1, one launch (start us, length us, event | category | flops | bytes accessed | tf_op | source)
XLA Modules:
  0.0 223.2 jit_solution(64430388502400549)
XLA Ops:
  6.5 0.0 copy-start
  6.5 0.0 copy-start.2
  6.5 0.0 copy-start.1
  6.5 0.0 all-gather.8.cloned.1.call-start
  6.5 0.7 all-gather.8.cloned.1.call-update
  7.3 0.0 all-gather.6.cloned.1.call-start
  7.3 0.8 copy-done
  8.1 1.0 copy.37
  9.1 0.0 all-gather.6.cloned.1.call-update
  9.1 0.0 all-gather.10.cloned.1.call-start
  9.2 0.7 dynamic-slice_convert_fusion
  9.9 0.7 select_reduce_fusion.1
  10.7 0.7 fusion.24
  11.4 0.3 multiply_cosine_fusion
  11.7 21.0 %all-gather.8.cloned.1.call-done = bf16[1,256,8192]{2,1,0:T(8,128)(2,1)} async-done(((bf16[1,128,8192]{2,1,0:T(8,128)(2,1)}), bf16[1,256,8192]{2,1,0:T(8,128)(2,1)}) %all-gather.8.cloned.1.call-update) | async-done | bytes 4194320 | tf_op jit(solution)/shard_map/all_gather | solution.py:52
  32.7 127.1 %all-gather.6.cloned.1.call-done = bf16[2,8192,256]{1,2,0:T(8,128)(2,1)} async-done(((bf16[2,512,256]{1,2,0:T(8,128)(2,1)}), bf16[2,8192,256]{1,2,0:T(8,128)(2,1)}) %all-gather.6.cloned.1.call-update) | async-done | bytes 8388624 | tf_op jit(solution)/shard_map/all_gather | solution.py:57
  159.8 6.9 %fusion.14 = f32[2,256,256]{1,2,0:T(8,128)S(1)} fusion(bf16[2,8192,256]{1,2,0:T(8,128)(2,1)} %all-gather.6.cloned.1.call-done, bf16[1,256,8192]{2,1,0:T(8,128)(2,1)} %all-gather.8.cloned.1.call-done, f32[2,256]{1,0:T(2,128)S(1)} %dynamic-slice_convert_fusion), kind=kOutput, calls=%fused_computation.12 | convolution fusion | flops 2147614720 | bytes 13109248 | tf_op jit(solution)/shard_map/td,cde->cte/dot_general | solution.py:54
  166.9 0.9 copy.26
  167.8 0.0 all-gather.10.cloned.1.call-update
  167.8 0.0 copy-done.1
  167.8 1.2 copy.38
  169.0 0.0 copy-done.2
  169.0 0.1 select_reduce_fusion.2
  169.1 0.1 select_reduce_fusion
  169.2 0.2 broadcast_compare_fusion
  169.4 24.6 %all-gather.10.cloned.1.call-done = bf16[16,256,256]{2,1,0:T(8,128)(2,1)} async-done(((bf16[2,256,256]{2,1,0:T(8,128)(2,1)}), bf16[16,256,256]{2,1,0:T(8,128)(2,1)}) %all-gather.10.cloned.1.call-update) | async-done | bytes 2097168 | tf_op jit(solution)/shard_map/all_gather | solution.py:68
  194.0 3.1 %copy.27 = bf16[4,2,2,256,256]{3,0,4,1,2:T(4,128)(2,1)S(1)} copy(bf16[4,2,2,256,256]{4,3,2,1,0:T(8,128)(2,1)} %bitcast.56) | data formatting | bytes 4194304 | tf_op jit(solution)/shard_map/reshape | solution.py:70
  197.1 2.1 fusion.28
  199.2 1.8 reshape.180
  201.0 1.8 reshape_squeeze.13
  202.8 4.1 %fusion = (f32[4,8,128]{2,1,0:T(8,128)S(1)}, f32[4,1024,128,8]{2,1,3,0:T(8,128)S(1)}) fusion(pred[128,1024]{0,1:T(8,128)(4,1)S(1)} %broadcast_compare_fusion, bf16[128,4,8,128]{3,2,1,0:T(8,128)(2,1)} %bitcast.55, bf16[1024,4,128]{0,2,1:T(8,128)(2,1)S(1)} %reshape_squeeze.13), kind=kOutput, calls=%fused_computation.2 | convolution fusion | flops 1086320640 | bytes 19021824 | tf_op jit(solution)/shard_map/tgjd,sgd->gjts/dot_general | solution.py:87
  206.9 4.1 %fusion.1 = f32[4,8,128]{2,1,0:T(8,128)S(1)} fusion(f32[4,1024,128,8]{2,1,3,0:T(8,128)S(1)} %get-tuple-element.12, f32[4,8,128]{2,1,0:T(8,128)S(1)} %broadcast_maximum_fusion, pred[128,1024]{0,1:T(8,128)(4,1)S(1)} %broadcast_compare_fusion), kind=kLoop, calls=%fused_computation.3 | loop fusion | flops 20967424 | bytes 16941056 | tf_op jit(solution)/shard_map/reduce_sum | solution.py:95
  211.0 4.3 %fusion.8 = bf16[128,4,8,128]{0,3,2,1:T(8,128)(2,1)S(1)} fusion(f32[4,1024,128,8]{2,1,3,0:T(8,128)S(1)} %get-tuple-element.12, f32[4,8,128]{2,1,0:T(8,128)S(1)} %broadcast_maximum_fusion, pred[128,1024]{0,1:T(8,128)(4,1)S(1)} %broadcast_compare_fusion, bf16[1024,4,128,1]{0,2,1,3:T(8,128)(2,1)S(1)} %reshape.180, f32[128,4,8]{0,2,1:T(8,128)S(1)} %bitcast.61), kind=kOutput, calls=%fused_computation.10 | convolution fusion | flops 1095761920 | bytes 19038208 | tf_op jit(solution)/shard_map/gjts,sgd->gjtd/dot_general | solution.py:96
  215.4 1.3 copy.31
  (12 shorter events, 0.2 us)
Async XLA Ops:
  6.5 1.5 copy-start
  6.5 162.5 %copy-start.2 = (s32[1,8]{1,0:T(1,128)S(1)}, s32[1,8]{1,0:T(1,128)}, u32[]{:S(2)}) copy-start(s32[1,8]{1,0:T(1,128)} %param.11) | copy-start | bytes 100
  6.5 161.3 %copy-start.1 = (bf16[1,128,4096]{2,1,0:T(8,128)(2,1)S(1)}, bf16[1,128,4096]{2,1,0:T(8,128)(2,1)}, u32[]{:S(2)}) copy-start(bf16[1,128,4096]{2,1,0:T(8,128)(2,1)} %param.7) | copy-start | bytes 3145732
  6.5 26.1 %all-gather.8.cloned.1.call-start = ((), (), s32[]{:S(2)}) async-start(), calls=%async_computation.1 | async-start | bytes 6291456 | tf_op jit(solution)/shard_map/all_gather | solution.py:52
  7.3 152.5 %all-gather.6.cloned.1.call-start = ((), (), s32[]{:S(2)}) async-start(), calls=%async_computation | async-start | bytes 8912896 | tf_op jit(solution)/shard_map/all_gather | solution.py:57
  9.1 184.9 %all-gather.10.cloned.1.call-start = ((), (), s32[]{:S(2)}) async-start(), calls=%async_computation.2 | async-start | bytes 2359296 | tf_op jit(solution)/shard_map/all_gather | solution.py:68
Sparse Core Ops, SparseCore 0:
  9.1 23.5 all-gather.7
  35.1 124.6 all-gather.5
  167.9 26.0 all-gather.9
where the time goes:
time: 223 us
  waiting for transfers between devices  173 us (78%)
  matrix products  15.3 us (7%)
  local copies, waits for them, and re-layouts  13.9 us (6%)
  between operations  13.3 us (6%)
  other arithmetic  7.09 us (3%)
    all_gather x1, waiting for transfers between devices, per_device(): lax.all_gather(w_part, FSDP, axis=1, tiled=True)  127 us
    all_gather x1, waiting for transfers between devices, per_device(): gathered = lax.all_gather(stacked, SEQ, axis=0, tiled=False)  24.6 us
    all_gather x1, waiting for transfers between devices, per_device(): chip_rows = lax.all_gather(hidden[0], 'sc', axis=0, tiled=True)  21 us
    dot_general x1, matrix products, per_device(): jnp.einsum('td,cde->cte', chip_rows, lax.all_gather(w_part, FSDP, axis=1,...  6.93 us
  transfers between devices with their start and end apart: 3, of which 3 were waited for; matrix products, arithmetic and copies ran while one was open for 2% of the time, Pallas kernels for 0%

commit v1 on v0

--- a/solution.py
+++ b/solution.py
@@ -43,6 +43,18 @@
 def make_per_device(cores):
 
     def per_device(hidden, queries, w_kv, b_kv, doc_starts, block_docs):
+
+        def create_pools(xs, ax_name, on_dim):
+            return jnp.concatenate(
+                lax.all_to_all(
+                    jnp.stack(lax.psum(1, axis_name=ax_name) * [xs], 0),
+                    axis_name=ax_name,
+                    split_axis=0,
+                    concat_axis=0,
+                ),
+                on_dim,
+            )
+
         tok_count = hidden.shape[1]
         core = lax.axis_index("sc")
         chip = lax.axis_index("sy")
@@ -54,7 +66,7 @@
         key_value = jnp.einsum(
             "td,cde->cte",
             chip_rows,
-            lax.all_gather(w_part, FSDP, axis=1, tiled=True),
+            create_pools(w_part, FSDP, 1),
             preferred_element_type=jnp.float32,
         )
         key_value = key_value + b_part.astype(jnp.float32)[:, None, :]

time: 223 us -> 296 us (1.33)
  waiting for transfers between devices: 173 us -> 214 us
  local copies, waits for them, and re-layouts: 13.9 us -> 27.2 us
  starting transfers between devices: 0.08 us -> 11.7 us
  matrix products: 15.3 us -> 20.3 us
    all_to_all x0 -> x1, waiting for transfers between devices: none -> 182 us  [create_pools(): lax.all_to_all(jnp.stack(lax.psum(1, axis_name=ax_name) * [xs], 0), axis_...]
    all_gather x1 -> x0, waiting for transfers between devices: 127 us -> none  [per_device(): lax.all_gather(w_part, FSDP, axis=1, tiled=True)]
    all_gather x1, waiting for transfers between devices: 21 us -> 0.01 us  [per_device(): chip_rows = lax.all_gather(hidden[0], 'sc', axis=0, tiled=True)]
    all_to_all x0 -> x1, starting transfers between devices: none -> 11.6 us  [create_pools(): lax.all_to_all(jnp.stack(lax.psum(1, axis_name=ax_name) * [xs], 0), axis_...]
    reshape x0 -> x1, local copies, waits for them, and re-layouts: none -> 7.92 us  [create_pools(): jnp.concatenate(lax.all_to_all(jnp.stack(lax.psum(1, axis_name=ax_name) *...]
    all_gather x1, waiting for transfers between devices: 24.6 us -> 31.8 us  [per_device(): gathered = lax.all_gather(stacked, SEQ, axis=0, tiled=False)]
    dot_general x1, matrix products: 4.07 us -> 9.03 us  [per_device(): jnp.einsum('tgjd,sgd->gjts', query_heads, key_part, preferred_element_typ...]
    another operation x0 -> x1, local copies, waits for them, and re-layouts: none -> 4.17 us  [create_pools(): jnp.stack(lax.psum(1, axis_name=ax_name) * [xs], 0)]
  transfers between devices with their start and end apart: 3 -> 3, of which waited for: 3 -> 2; matrix products, arithmetic and copies ran while one was open for 2% -> 3% of each run, Pallas kernels for 0% -> 0%
where the time goes in v1:
time: 296 us
  waiting for transfers between devices  214 us (72%)
  local copies, waits for them, and re-layouts  27.2 us (9%)
  matrix products  20.3 us (7%)
  between operations  13.6 us (5%)
  starting transfers between devices  11.7 us (4%)
  other arithmetic  9.2 us (3%)
    all_to_all x1, waiting for transfers between devices, create_pools(): lax.all_to_all(jnp.stack(lax.psum(1, axis_name=ax_name) * [xs], 0), axis_...  182 us
    all_gather x1, waiting for transfers between devices, per_device(): gathered = lax.all_gather(stacked, SEQ, axis=0, tiled=False)  31.8 us
    all_to_all x1, starting transfers between devices, create_pools(): lax.all_to_all(jnp.stack(lax.psum(1, axis_name=ax_name) * [xs], 0), axis_...  11.6 us
    dot_general x1, matrix products, per_device(): jnp.einsum('tgjd,sgd->gjts', query_heads, key_part, preferred_element_typ...  9.03 us
    reduce_sum x1, other arithmetic, per_device(): new_sum = jnp.sum(weight, axis=-1)  8.22 us
    reshape x1, local copies, waits for them, and re-layouts, create_pools(): jnp.concatenate(lax.all_to_all(jnp.stack(lax.psum(1, axis_name=ax_name) *...  7.92 us
    dot_general x1, matrix products, per_device(): jnp.einsum('td,cde->cte', chip_rows, create_pools(w_part, FSDP, 1), prefe...  6.94 us
  transfers between devices with their start and end apart: 3, of which 2 were waited for; matrix products, arithmetic and copies ran while one was open for 3% of the time, Pallas kernels for 0%

profile of v1, /device:TPU:1, one launch (start us, length us, event | category | flops | bytes accessed | tf_op | source)
XLA Modules:
  0.0 296.0 jit_solution(13538728447720755780)
XLA Ops:
  6.5 0.0 copy-start
  6.5 0.0 copy-start.5
  6.5 0.0 copy-start.4
  6.5 0.0 copy-start.6
  6.5 1.2 copy-done
  7.8 0.2 copy.26
  8.0 4.2 %stack.4 = bf16[16,2,512,256]{2,3,1,0:T(8,128)(2,1)} broadcast(bf16[2,512,256]{1,2,0:T(8,128)(2,1)S(1)} %copy.26), dimensions={1,2,3} | broadcast | bytes 8912896 | tf_op jit(solution)/shard_map/stack | solution.py:50
  12.2 11.6 %all-to-all-start = ((bf16[16,2,512,256]{2,3,1,0:T(8,128)(2,1)}), bf16[16,2,512,256]{2,3,1,0:T(8,128)(2,1)}, u32[]{:S(2)}, u32[]{:S(2)}) async-start(bf16[16,2,512,256]{2,3,1,0:T(8,128)(2,1)} %stack.4), calls=%async_computation | async-start | bytes 16777216 | tf_op jit(solution)/shard_map/all_to_all | solution.py:49
  23.8 0.0 all-gather.5.cloned.1.call-start
  23.9 0.7 all-gather.5.cloned.1.call-update
  24.5 0.0 all-gather.7.cloned.1.call-start
  24.6 0.0 copy-done.5
  24.7 0.0 copy-done.4
  24.7 0.1 select_reduce_fusion.1
  24.8 0.0 copy-done.6
  24.8 0.1 fusion.24
  24.8 0.3 multiply_cosine_fusion
  25.2 181.6 %all-to-all-done = bf16[16,2,512,256]{2,3,1,0:T(8,128)(2,1)} async-done(((bf16[16,2,512,256]{2,3,1,0:T(8,128)(2,1)}), bf16[16,2,512,256]{2,3,1,0:T(8,128)(2,1)}, u32[]{:S(2)}, u32[]{:S(2)}) %all-to-all-start) | async-done | bytes 8388640 | tf_op jit(solution)/shard_map/all_to_all | solution.py:49
  206.7 0.0 copy-start.3
  206.7 7.9 %copy.39 = bf16[16,2,32,8,512]{4,3,0,2,1:T(8,128)(2,1)} copy(bf16[16,2,32,8,512]{4,3,2,1,0:T(8,128)(2,1)} %bitcast.18) | data formatting | bytes 16777216 | tf_op jit(solution)/shard_map/reshape | solution.py:48
  214.7 0.0 all-gather.5.cloned.1.call-done
  214.7 6.9 %fusion.14 = f32[2,256,256]{1,2,0:T(8,128)S(1)} fusion(bf16[2,8192,256]{1,2,0:T(8,128)(2,1)} %bitcast.57, bf16[1,256,8192]{2,1,0:T(8,128)(2,1)} %all-gather.5.cloned.1.call-done, f32[2,256]{1,0:T(2,128)S(1)} %dynamic-slice_convert_fusion), kind=kOutput, calls=%fused_computation.12 | convolution fusion | flops 2147614720 | bytes 13109248 | tf_op jit(solution)/shard_map/td,cde->cte/dot_general | solution.py:66
  221.8 0.9 copy.28
  222.6 0.0 all-gather.7.cloned.1.call-update
  222.7 0.0 copy-done.3
  222.7 1.2 copy.40
  223.9 0.1 select_reduce_fusion.2
  224.0 0.1 select_reduce_fusion
  224.1 0.2 broadcast_compare_fusion
  224.3 31.8 %all-gather.7.cloned.1.call-done = bf16[16,256,256]{2,1,0:T(8,128)(2,1)} async-done(((bf16[2,256,256]{2,1,0:T(8,128)(2,1)}), bf16[16,256,256]{2,1,0:T(8,128)(2,1)}) %all-gather.7.cloned.1.call-update) | async-done | bytes 2097168 | tf_op jit(solution)/shard_map/all_gather | solution.py:80
  256.1 3.1 %copy.29 = bf16[4,2,2,256,256]{3,0,4,1,2:T(4,128)(2,1)S(1)} copy(bf16[4,2,2,256,256]{4,3,2,1,0:T(8,128)(2,1)} %bitcast.60) | data formatting | bytes 4194304 | tf_op jit(solution)/shard_map/reshape | solution.py:82
  259.1 2.1 fusion.28
  261.2 0.0 copy-start.2
  261.2 1.9 reshape_squeeze.13
  263.1 9.0 %fusion = (f32[4,8,128]{2,1,0:T(8,128)S(1)}, f32[4,1024,128,8]{2,1,3,0:T(8,128)}) fusion(pred[128,1024]{0,1:T(8,128)(4,1)S(1)} %broadcast_compare_fusion, bf16[128,4,8,128]{3,2,1,0:T(8,128)(2,1)} %bitcast.59, bf16[1024,4,128]{0,2,1:T(8,128)(2,1)S(1)} %reshape_squeeze.13), kind=kOutput, calls=%fused_computation.2 | convolution fusion | flops 1086320640 | bytes 19021824 | tf_op jit(solution)/shard_map/tgjd,sgd->gjts/dot_general | solution.py:99
  272.2 0.0 copy-done.2
  272.2 0.8 reshape.190
  272.9 0.0 copy-start.1
  273.0 8.2 %fusion.1 = f32[4,8,128]{2,1,0:T(8,128)S(1)} fusion(f32[4,1024,128,8]{2,1,3,0:T(8,128)} %get-tuple-element.12, f32[4,8,128]{2,1,0:T(8,128)S(1)} %broadcast_maximum_fusion, pred[128,1024]{0,1:T(8,128)(4,1)S(1)} %broadcast_compare_fusion), kind=kLoop, calls=%fused_computation.3 | loop fusion | flops 20967424 | bytes 16941056 | tf_op jit(solution)/shard_map/reduce_sum | solution.py:107
  281.2 2.4 copy-done.1
  283.6 4.3 %fusion.8 = bf16[128,4,8,128]{0,3,2,1:T(8,128)(2,1)S(1)} fusion(f32[4,1024,128,8]{2,1,3,0:T(8,128)S(1)} %copy-done.1, f32[4,8,128]{2,1,0:T(8,128)S(1)} %broadcast_maximum_fusion, pred[128,1024]{0,1:T(8,128)(4,1)S(1)} %broadcast_compare_fusion, bf16[1024,4,128,1]{0,2,1,3:T(8,128)(2,1)S(1)} %reshape.190, f32[128,4,8]{0,2,1:T(8,128)S(1)} %bitcast.65), kind=kOutput, calls=%fused_computation.10 | convolution fusion | flops 1095761920 | bytes 19038208 | tf_op jit(solution)/shard_map/gjts,sgd->gjtd/dot_general | solution.py:108
  287.9 1.3 copy.33
  (13 shorter events, 0.2 us)
Async XLA Ops:
  6.5 1.2 copy-start
  6.5 18.1 %copy-start.5 = (bf16[2,512]{1,0:T(2,128)(2,1)S(1)}, bf16[2,512]{1,0:T(2,128)(2,1)}, u32[]{:S(2)}) copy-start(bf16[2,512]{1,0:T(2,128)(2,1)} %param.9) | copy-start | bytes 6148
  6.5 18.1 %copy-start.4 = (s32[1,8]{1,0:T(1,128)S(1)}, s32[1,8]{1,0:T(1,128)}, u32[]{:S(2)}) copy-start(s32[1,8]{1,0:T(1,128)} %param.11) | copy-start | bytes 100
  6.5 18.2 %copy-start.6 = (s32[1,2]{1,0:T(1,128)S(1)}, s32[1,2]{1,0:T(1,128)}, u32[]{:S(2)}) copy-start(s32[1,2]{1,0:T(1,128)} %param.10) | copy-start | bytes 28
  12.2 194.6 %all-to-all-start = ((bf16[16,2,512,256]{2,3,1,0:T(8,128)(2,1)}), bf16[16,2,512,256]{2,3,1,0:T(8,128)(2,1)}, u32[]{:S(2)}, u32[]{:S(2)}) async-start(bf16[16,2,512,256]{2,3,1,0:T(8,128)(2,1)} %stack.4), calls=%async_computation | async-start | bytes 16777216 | tf_op jit(solution)/shard_map/all_to_all | solution.py:49
  23.8 190.9 %all-gather.5.cloned.1.call-start = ((), (), s32[]{:S(2)}) async-start(), calls=%async_computation.1 | async-start | bytes 6291456 | tf_op jit(solution)/shard_map/all_gather | solution.py:64
  24.5 231.5 %all-gather.7.cloned.1.call-start = ((), (), s32[]{:S(2)}) async-start(), calls=%async_computation.2 | async-start | bytes 2359296 | tf_op jit(solution)/shard_map/all_gather | solution.py:80
  206.7 15.9 %copy-start.3 = (bf16[1,128,4096]{2,1,0:T(8,128)(2,1)S(1)}, bf16[1,128,4096]{2,1,0:T(8,128)(2,1)}, u32[]{:S(2)}) copy-start(bf16[1,128,4096]{2,1,0:T(8,128)(2,1)} %param.7) | copy-start | bytes 3145732
  261.2 10.9 %copy-start.2 = (bf16[1,4,256,2,256]{2,1,4,3,0:T(4,128)(2,1)S(1)}, bf16[1,4,256,2,256]{2,1,4,3,0:T(4,128)(2,1)}, u32[]{:S(2)}) copy-start(bf16[1,4,256,2,256]{2,1,4,3,0:T(4,128)(2,1)} %get-tuple-element.5) | copy-start | bytes 3145732
  272.9 10.6 %copy-start.1 = (f32[4,1024,128,8]{2,1,3,0:T(8,128)S(1)}, f32[4,1024,128,8]{2,1,3,0:T(8,128)}, u32[]{:S(2)}) copy-start(f32[4,1024,128,8]{2,1,3,0:T(8,128)} %get-tuple-element.12) | copy-start | bytes 50331652
Sparse Core Ops, SparseCore 0:
  26.4 21.4 all-gather.4
  222.8 33.2 all-gather.6
